TPU v7x, 256 devices: a whole 4x4x8 slice. The times are simulated.
256 devices in a mesh: anim: 16 (over y, x_lo, core), snp: 16 (over z, x_hi).
Axes of the slice: x: 4 (x_hi: 2, x_lo: 2; x = x_hi * 2 + x_lo), y: 4, z: 8, core: 2. Of those that a mesh axis runs over, the one named last changes fastest.
Arguments:
- core_geno: bfloat16 [12288, 49152], P('anim', 'snp'), may hold values from -10 to 10, as said below
- noncore_geno: bfloat16 [12288, 49152], P('anim', 'snp'), may hold values from -10 to 10, as said below
- core_inv: bfloat16 [12288, 12288], P('anim', 'snp'), may hold values from -0.0546875 to 0.0546875
- snp_effects: bfloat16 [256, 49152], P(None, 'snp'), may hold values from -0.02734375 to 0.02734375
- noncore_scale: float32 [12288], P('anim'), may hold values from 0.5 to 2
Outputs:
- noncore_out: float32 [256, 12288], P(None, 'anim')
- core_out: float32 [256, 12288], P(None, ('anim', 'snp'))
Inputs may be any that keep to these rules, and one draw needn't show every extreme that they name: `core_geno`: each column j is (c - 2 p_j) / sqrt(2 p_j (1 - p_j)) for codes c in 0, 1, 2 and a column frequency p_j shared with noncore_geno. `noncore_geno`: each column j is (c - 2 p_j) / sqrt(2 p_j (1 - p_j)) for codes c in 0, 1, 2 and a column frequency p_j shared with core_geno.
All inputs are finite; a program needn't handle non-finite values.
Results may differ from a plain program's by a relative error of at most 0.008.
Values may be sent and summed in bfloat16 or wider, within the bound.
A program may use at most 64 MiB of HBM per device.

v0:
```python
import jax
import jax.numpy as jnp
from jax import lax
from jax.sharding import PartitionSpec as P

NSNP = 49152


def contract_last(left, right):
    return lax.dot_general(
        left, right, (((1,), (1,)), ((), ())), preferred_element_type=jnp.float32
    )


def core_columns(partial_value, base, tile_cols):
    snp_index = lax.axis_index("snp")
    summed = lax.psum(partial_value, "snp")
    value = summed if base is None else base.astype(jnp.float32) - summed
    block = value.astype(jnp.bfloat16)
    whole = lax.all_gather(block, "anim", axis=1, tiled=True)
    columns = lax.dynamic_slice_in_dim(whole, snp_index * tile_cols, tile_cols, 1)
    return (block, columns)


def marker_terms(partial_value):
    total = lax.psum(partial_value, "anim")
    return (total / NSNP).astype(jnp.bfloat16)


def local(core_geno, noncore_geno, core_inv, snp_effects, noncore_scale):
    tile_cols = core_inv.shape[1]
    core_partial = contract_last(snp_effects, core_geno)
    noncore_partial = contract_last(snp_effects, noncore_geno)
    core_vals, value_cols = core_columns(core_partial, None, tile_cols)
    noncore_vals = lax.psum(noncore_partial, "snp")
    weight_partial = contract_last(value_cols, core_inv)
    core_weights = lax.psum(weight_partial, "snp").astype(jnp.bfloat16)
    snp_core = marker_terms(jnp.dot(core_weights, core_geno, preferred_element_type=jnp.float32))
    predicted = lax.psum(contract_last(snp_core, noncore_geno), "snp")
    noncore_out = noncore_scale[None, :] * (noncore_vals - predicted)
    noncore_half = noncore_out.astype(jnp.bfloat16)
    snp_noncore = marker_terms(
        jnp.dot(noncore_half, noncore_geno, preferred_element_type=jnp.float32)
    )
    back_partial = contract_last(snp_noncore, core_geno)
    core_rest, rest_cols = core_columns(back_partial, core_vals, tile_cols)
    out_partial = contract_last(rest_cols, core_inv)
    core_out = lax.psum_scatter(out_partial, "snp", scatter_dimension=1, tiled=True)
    return (noncore_out, core_out)


def solution(mesh):
    return jax.shard_map(
        local,
        mesh=mesh,
        in_specs=(P("anim", "snp"), P("anim", "snp"), P("anim", "snp"), P(None, "snp"), P("anim")),
        out_specs=(P(None, "anim"), P(None, ("anim", "snp"))),
        check_vma=False,
    )
```

profile of v0, /device:TPU:8, one launch (start us, length us, event | category | flops | bytes accessed | tf_op | source)
XLA Modules:
  0.0 1105.2 jit_solution(17298598876535657185)
XLA Ops:
  7.2 0.0 copy-start
  7.2 0.0 copy-start.2
  7.2 0.0 all-gather.3.cloned.1.call-start
  7.2 1.3 copy-done
  8.6 3.8 fusion.17
  12.3 89.5 %all-reduce.15 = bf16[256,768]{1,0:T(8,128)(2,1)} all-reduce(f32[256,768]{1,0:T(8,128)S(1)} %fusion.17), channel_id=1, replica_groups=mesh['anim'=16,'snp'=16] {'snp'}, use_global_device_ids=true, to_apply=%region_1.0 | all-reduce | flops 196608 | bytes 1179648 | tf_op jit(solution)/shard_map/psum | solution.py:17
  101.8 0.0 all-gather.3.cloned.1.call-update
  101.9 0.0 all-reduce.8.cloned.1.call-start
  101.9 40.4 %all-gather.3.cloned.1.call-done = bf16[256,12288]{1,0:T(8,128)(2,1)} async-done(((bf16[256,768]{1,0:T(8,128)(2,1)}), bf16[256,12288]{1,0:T(8,128)(2,1)}) %all-gather.3.cloned.1.call-update) | async-done | bytes 6291472 | tf_op jit(solution)/shard_map/all_gather | solution.py:20
  142.3 0.0 copy-done.2
  142.3 1.5 fusion.10
  143.8 87.3 %all-reduce.16 = bf16[256,768]{1,0:T(8,128)(2,1)} all-reduce(f32[256,768]{1,0:T(8,128)S(1)} %fusion.10), channel_id=1, replica_groups=mesh['anim'=16,'snp'=16] {'snp'}, use_global_device_ids=true, to_apply=%region_2.0 | all-reduce | flops 196608 | bytes 1179648 | tf_op jit(solution)/shard_map/psum | solution.py:37
  231.1 5.5 fusion.18
  236.6 0.0 all-reduce.8.cloned.1.call-update
  236.6 0.0 all-reduce.14.cloned.1.call-start
  236.7 4.6 fusion.16
  241.3 0.0 copy-start.4
  241.3 121.1 %all-reduce.8.cloned.1.call-done = f32[256,3072]{1,0:T(8,128)} async-done(((f32[256,3072]{1,0:T(8,128)}), f32[256,3072]{1,0:T(8,128)}) %all-reduce.8.cloned.1.call-update) | async-done | bytes 3145744 | tf_op jit(solution)/shard_map/psum | solution.py:26
  362.4 5.6 fusion
  368.0 0.0 all-reduce.14.cloned.1.call-update
  368.0 0.0 all-reduce.10.cloned.1.call-start
  368.1 169.1 %all-reduce.14.cloned.1.call-done = (f32[256,768]{1,0:T(8,128)}, f32[256,768]{1,0:T(8,128)}) async-done(((f32[256,768]{1,0:T(8,128)}, f32[256,768]{1,0:T(8,128)}), (f32[256,768]{1,0:T(8,128)}, f32[256,768]{1,0:T(8,128)})) %all-reduce.14.cloned.1.call-update) | async-done | bytes 1572880 | tf_op jit(solution)/shard_map/psum | solution.py:35
  537.1 0.0 copy-done.4
  537.1 1.5 subtract_multiply_fusion
  538.6 0.0 copy-start.1
  538.6 5.7 fusion.6
  544.3 0.0 copy-done.1
  544.3 0.0 all-reduce.10.cloned.1.call-update
  544.3 0.0 copy-start.3
  544.4 0.0 all-reduce.12.cloned.1.call-start
  544.4 128.0 %all-reduce.10.cloned.1.call-done = f32[256,3072]{1,0:T(8,128)} async-done(((f32[256,3072]{1,0:T(8,128)}), f32[256,3072]{1,0:T(8,128)}) %all-reduce.10.cloned.1.call-update) | async-done | bytes 3145744 | tf_op jit(solution)/shard_map/psum | solution.py:26
  672.4 5.6 fusion.1
  678.0 0.0 all-reduce.12.cloned.1.call-update
  678.0 0.0 all-gather.5.cloned.1.call-start
  678.0 165.4 %all-reduce.12.cloned.1.call-done = f32[256,768]{1,0:T(8,128)} async-done(((f32[256,768]{1,0:T(8,128)}), f32[256,768]{1,0:T(8,128)}) %all-reduce.12.cloned.1.call-update) | async-done | bytes 786448 | tf_op jit(solution)/shard_map/psum | solution.py:17
  843.4 0.0 copy-done.3
  843.4 1.9 subtract_convert_fusion
  845.4 0.0 all-gather.5.cloned.1.call-update
  845.4 0.0 reduce-scatter.2.cloned.1.call-start
  845.4 42.9 %all-gather.5.cloned.1.call-done = bf16[256,12288]{1,0:T(8,128)(2,1)} async-done(((bf16[256,768]{1,0:T(8,128)(2,1)}), bf16[256,12288]{1,0:T(8,128)(2,1)}) %all-gather.5.cloned.1.call-update) | async-done | bytes 6291472 | tf_op jit(solution)/shard_map/all_gather | solution.py:20
  888.4 2.4 fusion.4
  890.7 0.0 reduce-scatter.2.cloned.1.call-update
  890.8 207.5 %reduce-scatter.2.cloned.1.call-done = f32[256,48]{0,1:T(8,128)} async-done(((f32[256,768]{0,1:T(8,128)}), f32[256,48]{0,1:T(8,128)}) %reduce-scatter.2.cloned.1.call-update) | async-done | bytes 49168 | tf_op jit(solution)/shard_map/reduce_scatter | solution.py:48
Async XLA Ops:
  7.2 1.4 copy-start
  7.2 135.1 %copy-start.2 = (bf16[768,768]{1,0:T(8,128)(2,1)S(1)}, bf16[768,768]{1,0:T(8,128)(2,1)}, u32[]{:S(2)}) copy-start(bf16[768,768]{1,0:T(8,128)(2,1)} %param.7) | copy-start | bytes 3538948
  7.2 135.1 %all-gather.3.cloned.1.call-start = ((), (), s32[]{:S(2)}) async-start(), calls=%async_computation.1 | async-start | bytes 6684672 | tf_op jit(solution)/shard_map/all_gather | solution.py:20
  101.9 260.6 %all-reduce.8.cloned.1.call-start = ((), (), s32[]{:S(2)}) async-start(), calls=%async_computation.2 | async-start | bytes 6291456 | tf_op jit(solution)/shard_map/psum | solution.py:26
  236.6 300.5 %all-reduce.14.cloned.1.call-start = ((), (), s32[]{:S(2)}) async-start(), calls=%async_computation.7 | async-start | bytes 3145728 | tf_op jit(solution)/shard_map/psum | solution.py:35
  241.3 295.8 %copy-start.4 = (f32[768]{0:T(1024)S(1)}, f32[768]{0:T(1024)}, u32[]{:S(2)}) copy-start(f32[768]{0:T(1024)} %param.9) | copy-start | bytes 9220
  368.0 304.3 %all-reduce.10.cloned.1.call-start = ((), (), s32[]{:S(2)}) async-start(), calls=%async_computation.3 | async-start | bytes 6291456 | tf_op jit(solution)/shard_map/psum | solution.py:26
  538.6 5.7 copy-start.1
  544.3 299.1 %copy-start.3 = (bf16[256,768]{1,0:T(8,128)(2,1)S(1)}, bf16[256,768]{1,0:T(8,128)(2,1)}, u32[]{:S(2)}) copy-start(bf16[256,768]{1,0:T(8,128)(2,1)} %all-reduce.15) | copy-start | bytes 1179652
  544.4 299.1 %all-reduce.12.cloned.1.call-start = ((), (), s32[]{:S(2)}) async-start(), calls=%async_computation.4 | async-start | bytes 1572864 | tf_op jit(solution)/shard_map/psum | solution.py:17
  678.0 210.4 %all-gather.5.cloned.1.call-start = ((), (), s32[]{:S(2)}) async-start(), calls=%async_computation.5 | async-start | bytes 6684672 | tf_op jit(solution)/shard_map/all_gather | solution.py:20
  845.4 252.9 %reduce-scatter.2.cloned.1.call-start = ((), (), s32[]{:S(2)}) async-start(), calls=%async_computation.6 | async-start | bytes 835584 | tf_op jit(solution)/shard_map/reduce_scatter | solution.py:48
Sparse Core Ops, SparseCore 0:
  102.0 40.2 all-gather.2
  236.8 125.6 all-reduce.7
  368.2 168.9 all-reduce.13
  544.5 127.8 all-reduce.9
  678.1 165.2 all-reduce.11
  845.5 42.8 all-gather.4
  892.8 205.5 reduce-scatter.1
where the time goes:
time: 1110 us
  waiting for transfers between devices  874 us (79%)
  blocking collectives  177 us (16%)
  matrix products  34.7 us (3%)
  between operations  14.2 us (1%)
    psum x2, waiting for transfers between devices, marker_terms(): total = lax.psum(partial_value, 'anim')  249 us
    reduce_scatter x1, waiting for transfers between devices, local(): lax.psum_scatter(out_partial, 'snp', scatter_dimension=1, tiled=True)  208 us
    psum x1, waiting for transfers between devices, local(): noncore_vals = lax.psum(noncore_partial, 'snp')  169 us
    psum x1, waiting for transfers between devices, core_columns(): summed = lax.psum(partial_value, 'snp')  165 us
    psum x1, blocking collectives, core_columns(): summed = lax.psum(partial_value, 'snp')  89.5 us
    psum x1, blocking collectives, local(): core_weights = lax.psum(weight_partial, 'snp').astype(jnp.bfloat16)  87.3 us
    all_gather x2, waiting for transfers between devices, core_columns(): whole = lax.all_gather(block, 'anim', axis=1, tiled=True)  83.3 us
    dot_general x6, matrix products, contract_last(): lax.dot_general(left, right, (((1,), (1,)), ((), ())), preferred_element_...  23.5 us
  transfers between devices with their start and end apart: 7, of which 7 were waited for; matrix products, arithmetic and copies ran while one was open for 0% of the time, Pallas kernels for 0%

commit v1 on v0

--- a/solution.py
+++ b/solution.py
@@ -17,7 +17,10 @@
     summed = lax.psum(partial_value, "snp")
     value = summed if base is None else base.astype(jnp.float32) - summed
     block = value.astype(jnp.bfloat16)
-    whole = lax.all_gather(block, "anim", axis=1, tiled=True)
+    n_dev = lax.axis_size("anim")
+    blocks = jnp.stack([block for _ in range(n_dev)])
+    blocks = lax.all_to_all(blocks, "anim", split_axis=0, concat_axis=0)
+    whole = jnp.concatenate(blocks, axis=1)
     columns = lax.dynamic_slice_in_dim(whole, snp_index * tile_cols, tile_cols, 1)
     return (block, columns)
 

time: 1110 us -> 1170 us (1.054)
  blocking collectives: 177 us -> 246 us
  waiting for transfers between devices: 874 us -> 859 us
    all_gather x2 -> x0, waiting for transfers between devices: 83.3 us -> none  [core_columns(): whole = lax.all_gather(block, 'anim', axis=1, tiled=True)]
    all_to_all x0 -> x1, blocking collectives: none -> 75.2 us  [core_columns(): blocks = lax.all_to_all(blocks, 'anim', split_axis=0, concat_axis=0)]
    all_to_all x0 -> x1, waiting for transfers between devices: none -> 71.2 us  [core_columns(): blocks = lax.all_to_all(blocks, 'anim', split_axis=0, concat_axis=0)]
  transfers between devices with their start and end apart: 7 -> 6, of which waited for: 7 -> 6; matrix products, arithmetic and copies ran while one was open for 0% -> 0% of each run, Pallas kernels for 0% -> 0%
where the time goes in v1:
time: 1170 us
  waiting for transfers between devices  859 us (73%)
  blocking collectives  246 us (21%)
  matrix products  33.7 us (3%)
  between operations  13.9 us (1%)
    psum x2, waiting for transfers between devices, marker_terms(): total = lax.psum(partial_value, 'anim')  251 us
    reduce_scatter x1, waiting for transfers between devices, local(): lax.psum_scatter(out_partial, 'snp', scatter_dimension=1, tiled=True)  203 us
    psum x1, waiting for transfers between devices, local(): noncore_vals = lax.psum(noncore_partial, 'snp')  169 us
    psum x1, waiting for transfers between devices, core_columns(): summed = lax.psum(partial_value, 'snp')  165 us
    psum x1, blocking collectives, core_columns(): summed = lax.psum(partial_value, 'snp')  89 us
    psum x1, blocking collectives, local(): core_weights = lax.psum(weight_partial, 'snp').astype(jnp.bfloat16)  82.3 us
    all_to_all x1, blocking collectives, core_columns(): blocks = lax.all_to_all(blocks, 'anim', split_axis=0, concat_axis=0)  75.2 us
    all_to_all x1, waiting for transfers between devices, core_columns(): blocks = lax.all_to_all(blocks, 'anim', split_axis=0, concat_axis=0)  71.2 us
  transfers between devices with their start and end apart: 6, of which 6 were waited for; matrix products, arithmetic and copies ran while one was open for 0% of the time, Pallas kernels for 0%

profile of v1, /device:TPU:8, one launch (start us, length us, event | category | flops | bytes accessed | tf_op | source)
XLA Modules:
  0.0 1168.0 jit_solution(14101851491667162387)
XLA Ops:
  7.2 0.0 copy-start
  7.2 1.4 copy-done
  8.6 3.7 fusion.17
  12.3 89.0 %all-reduce.15 = bf16[256,768]{1,0:T(8,128)(2,1)S(1)} all-reduce(f32[256,768]{1,0:T(8,128)S(1)} %fusion.17), channel_id=1, replica_groups=mesh['anim'=16,'snp'=16] {'snp'}, use_global_device_ids=true, to_apply=%region_1.0 | all-reduce | flops 196608 | bytes 1179648 | tf_op jit(solution)/shard_map/psum | solution.py:17
  101.4 0.0 copy-start.3
  101.4 0.2 copy.7
  101.6 0.6 copy-done.3
  102.1 3.3 stack.4
  105.4 0.0 copy-start.2
  105.4 5.7 all-to-all-start
  111.1 0.0 all-reduce.8.cloned.1.call-start
  111.1 71.2 %all-to-all-done = bf16[16,256,768]{1,2,0:T(8,128)(2,1)} async-done(((bf16[16,256,768]{1,2,0:T(8,128)(2,1)}), bf16[16,256,768]{1,2,0:T(8,128)(2,1)}, u32[]{:S(2)}, u32[]{:S(2)}) %all-to-all-start) | async-done | bytes 6291488 | tf_op jit(solution)/shard_map/all_to_all | solution.py:22
  182.3 0.0 copy-done.2
  182.3 1.5 fusion.10
  183.8 82.3 %all-reduce.16 = bf16[256,768]{1,0:T(8,128)(2,1)} all-reduce(f32[256,768]{1,0:T(8,128)S(1)} %fusion.10), channel_id=1, replica_groups=mesh['anim'=16,'snp'=16] {'snp'}, use_global_device_ids=true, to_apply=%region_2.0 | all-reduce | flops 196608 | bytes 1179648 | tf_op jit(solution)/shard_map/psum | solution.py:40
  266.1 5.5 fusion.18
  271.6 0.0 all-reduce.8.cloned.1.call-update
  271.7 0.0 all-reduce.14.cloned.1.call-start
  271.7 4.6 fusion.16
  276.4 0.0 copy-start.5
  276.4 123.2 %all-reduce.8.cloned.1.call-done = f32[256,3072]{1,0:T(8,128)} async-done(((f32[256,3072]{1,0:T(8,128)}), f32[256,3072]{1,0:T(8,128)}) %all-reduce.8.cloned.1.call-update) | async-done | bytes 3145744 | tf_op jit(solution)/shard_map/psum | solution.py:29
  399.6 5.6 fusion
  405.2 0.0 all-reduce.14.cloned.1.call-update
  405.2 0.0 all-reduce.10.cloned.1.call-start
  405.2 169.0 %all-reduce.14.cloned.1.call-done = (f32[256,768]{1,0:T(8,128)}, f32[256,768]{1,0:T(8,128)}) async-done(((f32[256,768]{1,0:T(8,128)}, f32[256,768]{1,0:T(8,128)}), (f32[256,768]{1,0:T(8,128)}, f32[256,768]{1,0:T(8,128)})) %all-reduce.14.cloned.1.call-update) | async-done | bytes 1572880 | tf_op jit(solution)/shard_map/psum | solution.py:38
  574.3 0.0 copy-done.5
  574.3 1.5 subtract_multiply_fusion
  575.7 0.0 copy-start.1
  575.8 5.7 fusion.6
  581.4 0.0 copy-done.1
  581.4 0.0 all-reduce.10.cloned.1.call-update
  581.5 0.0 copy-start.4
  581.5 0.0 all-reduce.12.cloned.1.call-start
  581.5 127.6 %all-reduce.10.cloned.1.call-done = f32[256,3072]{1,0:T(8,128)} async-done(((f32[256,3072]{1,0:T(8,128)}), f32[256,3072]{1,0:T(8,128)}) %all-reduce.10.cloned.1.call-update) | async-done | bytes 3145744 | tf_op jit(solution)/shard_map/psum | solution.py:29
  709.1 5.6 fusion.1
  714.7 0.0 all-reduce.12.cloned.1.call-update
  714.7 0.0 reduce-scatter.2.cloned.1.call-start
  714.8 165.4 %all-reduce.12.cloned.1.call-done = f32[256,768]{1,0:T(8,128)} async-done(((f32[256,768]{1,0:T(8,128)}), f32[256,768]{1,0:T(8,128)}) %all-reduce.12.cloned.1.call-update) | async-done | bytes 786448 | tf_op jit(solution)/shard_map/psum | solution.py:17
  880.1 0.0 copy-done.4
  880.1 1.2 subtract_convert_fusion
  881.4 0.2 copy.8
  881.5 0.6 stack.5
  882.1 75.2 %all_to_all.10 = bf16[16,256,768]{1,2,0:T(8,128)(2,1)S(1)} all-to-all(bf16[16,256,768]{1,2,0:T(8,128)(2,1)S(1)} %stack.5), channel_id=1, replica_groups=mesh['anim'=16,'snp'=16] {'anim'}, dimensions={0} | all-to-all | bytes 12582912 | tf_op jit(solution)/shard_map/all_to_all | solution.py:22
  957.3 1.4 fusion.4
  958.7 0.0 reduce-scatter.2.cloned.1.call-update
  958.7 202.8 %reduce-scatter.2.cloned.1.call-done = f32[256,48]{0,1:T(8,128)} async-done(((f32[256,768]{0,1:T(8,128)}), f32[256,48]{0,1:T(8,128)}) %reduce-scatter.2.cloned.1.call-update) | async-done | bytes 49168 | tf_op jit(solution)/shard_map/reduce_scatter | solution.py:51
Async XLA Ops:
  7.2 1.4 copy-start
  101.4 0.8 copy-start.3
  105.4 77.0 %copy-start.2 = (bf16[768,768]{1,0:T(8,128)(2,1)S(1)}, bf16[768,768]{1,0:T(8,128)(2,1)}, u32[]{:S(2)}) copy-start(bf16[768,768]{1,0:T(8,128)(2,1)} %param.7) | copy-start | bytes 3538948
  105.4 77.0 %all-to-all-start = ((bf16[16,256,768]{1,2,0:T(8,128)(2,1)}), bf16[16,256,768]{1,2,0:T(8,128)(2,1)}, u32[]{:S(2)}, u32[]{:S(2)}) async-start(bf16[16,256,768]{1,2,0:T(8,128)(2,1)} %stack.4), calls=%async_computation | async-start | bytes 12582912 | tf_op jit(solution)/shard_map/all_to_all | solution.py:22
  111.1 288.5 %all-reduce.8.cloned.1.call-start = ((), (), s32[]{:S(2)}) async-start(), calls=%async_computation.3 | async-start | bytes 6291456 | tf_op jit(solution)/shard_map/psum | solution.py:29
  271.7 302.6 %all-reduce.14.cloned.1.call-start = ((), (), s32[]{:S(2)}) async-start(), calls=%async_computation.7 | async-start | bytes 3145728 | tf_op jit(solution)/shard_map/psum | solution.py:38
  276.4 297.9 %copy-start.5 = (f32[768]{0:T(1024)S(1)}, f32[768]{0:T(1024)}, u32[]{:S(2)}) copy-start(f32[768]{0:T(1024)} %param.9) | copy-start | bytes 9220
  405.2 303.9 %all-reduce.10.cloned.1.call-start = ((), (), s32[]{:S(2)}) async-start(), calls=%async_computation.4 | async-start | bytes 6291456 | tf_op jit(solution)/shard_map/psum | solution.py:29
  575.7 5.7 copy-start.1
  581.5 298.7 %copy-start.4 = (bf16[256,768]{1,0:T(8,128)(2,1)S(1)}, bf16[256,768]{1,0:T(8,128)(2,1)}, u32[]{:S(2)}) copy-start(bf16[256,768]{1,0:T(8,128)(2,1)} %copy-done.3) | copy-start | bytes 1179652
  581.5 298.7 %all-reduce.12.cloned.1.call-start = ((), (), s32[]{:S(2)}) async-start(), calls=%async_computation.5 | async-start | bytes 1572864 | tf_op jit(solution)/shard_map/psum | solution.py:17
  714.7 446.8 %reduce-scatter.2.cloned.1.call-start = ((), (), s32[]{:S(2)}) async-start(), calls=%async_computation.6 | async-start | bytes 835584 | tf_op jit(solution)/shard_map/reduce_scatter | solution.py:51
Sparse Core Ops, SparseCore 0:
  271.8 127.7 all-reduce.7
  405.3 168.9 all-reduce.13
  581.6 127.4 all-reduce.9
  714.8 165.2 all-reduce.11
  958.8 202.6 reduce-scatter.1
